TPU v7x, 32 devices: a whole 2x2x4 slice. The times are simulated.
32 devices in a mesh: design: 2 (over y), space: 8 (over z, x), case: 2 (over core).
Axes of the slice: x: 2, y: 2, z: 4, core: 2. Of those that a mesh axis runs over, the one named last changes fastest.
Arguments:
- displacement: float32 [16, 3, 96, 16, 128], P(('design', 'case'), None, 'space'), parts along dimension 0, may hold values from -3 to 3
- forces: float32 [16, 3, 96, 16, 128], P(('design', 'case'), None, 'space'), parts along dimension 0, may hold values from -13.6 to 13.6
- density: float32 [192, 16, 128], P(('design', 'space')), parts along dimension 0, may hold values from 0.1 to 1
- support_mask: int32 [192, 16, 128], P(('design', 'space')), parts along dimension 0, may hold values 0 or 1
- void_mask: int32 [192, 16, 128], P(('design', 'space')), parts along dimension 0, may hold values 0 or 1
Outputs:
- smoothed: float32 [16, 3, 96, 16, 128], P(('design', 'case'), None, 'space'), parts along dimension 0
- new_density: float32 [192, 16, 128], P(('design', 'space')), parts along dimension 0
- ks_value: float32 [2], P('design'), parts along dimension 0
There are 2 independent parts, one for each index of `design`. A program takes and returns all parts, laid end to end along the dimension named above; each array names one. Nothing has to cross between parts.
All inputs are finite; a program needn't handle non-finite values. No bound on the sum of `support_mask` or of `void_mask` on one device may be relied on, other than what follows from the above.
Results may differ from a plain program's by a relative error of at most 0.00002.
Values sent between devices are 32-bit elements; how exact they have to be, the bound alone decides.
A program may use at most 64 MiB of HBM per device.

v0:
```python
import math
import jax
import jax.numpy as jnp
from jax import lax
from jax.sharding import PartitionSpec as P

STIFF_MIN = 0.001
DIAG_SHIFT = 0.5
KS_BETA = 8.0
MOVE_LIMIT = 0.2
DENSITY_MIN = 0.001
STEP_ONE = 1.0 / (1.15 + 0.85 * math.cos(math.pi / 4))
STEP_TWO = 1.0 / (1.15 - 0.85 * math.cos(math.pi / 4))


def with_halo(block, sides, width):
    for axis, dim in sides:
        count = lax.axis_size(axis)
        forward = [(i, i + 1) for i in range(count - 1)]
        backward = [(target, source) for source, target in forward]
        low = lax.ppermute(
            lax.slice_in_dim(block, block.shape[dim] - width, None, axis=dim), axis, forward
        )
        high = lax.ppermute(lax.slice_in_dim(block, 0, width, axis=dim), axis, backward)
        block = jnp.concatenate([low, block, high], axis=dim)
    return block


def pad_axis(values, axis, width):
    widths = [(0, 0)] * values.ndim
    widths[values.ndim + axis] = (width, width)
    return jnp.pad(values, widths)


def stencil(fields, cube):
    face_x = STIFF_MIN + 0.5 * (cube[:-1] + cube[1:])
    middle = cube[1:-1]
    cube_y = pad_axis(middle, -2, 1)
    face_y = STIFF_MIN + 0.5 * (cube_y[:, :-1] + cube_y[:, 1:])
    cube_z = pad_axis(middle, -1, 1)
    face_z = STIFF_MIN + 0.5 * (cube_z[:, :, :-1] + cube_z[:, :, 1:])
    centre = fields[..., 1:-1, :, :]
    padded_y = pad_axis(centre, -2, 1)
    padded_z = pad_axis(centre, -1, 1)
    fluxes = face_x[1:] * (centre - fields[..., 2:, :, :]) + face_x[:-1] * (
        centre - fields[..., :-2, :, :]
    )
    fluxes = (
        fluxes
        + face_y[:, 1:] * (centre - padded_y[..., 2:, :])
        + face_y[:, :-1] * (centre - padded_y[..., :-2, :])
    )
    fluxes = (
        fluxes
        + face_z[:, :, 1:] * (centre - padded_z[..., 2:])
        + face_z[:, :, :-1] * (centre - padded_z[..., :-2])
    )
    diagonal = (
        DIAG_SHIFT
        + face_x[1:]
        + face_x[:-1]
        + face_y[:, 1:]
        + face_y[:, :-1]
        + face_z[:, :, 1:]
        + face_z[:, :, :-1]
    )
    return (DIAG_SHIFT * centre + fluxes, diagonal)


def smooth_sweep(fields, loads, cube, keep, factor):
    applied, diagonal = stencil(fields, cube)
    centre = fields[..., 1:-1, :, :]
    return keep * (centre + factor * (loads - applied) / diagonal)


def energy(extended, density):
    centre = extended[..., 1:-1, :, :]
    padded_y = pad_axis(centre, -2, 1)
    padded_z = pad_axis(centre, -1, 1)
    squares = (centre - extended[..., 2:, :, :]) ** 2 + (centre - extended[..., :-2, :, :]) ** 2
    squares = squares + (centre - padded_y[..., 2:, :]) ** 2 + (centre - padded_y[..., :-2, :]) ** 2
    squares = squares + (centre - padded_z[..., 2:]) ** 2 + (centre - padded_z[..., :-2]) ** 2
    return -1.5 * density * density * jnp.sum(squares, axis=-4)


def face_rim(motion):
    return with_halo(motion, (("space", 2),), 1)


def body(displacement, forces, density, support_mask, void_mask):
    planes = density.shape[0]
    rows_y = density.shape[1]
    rows_z = density.shape[2]
    slab_index = lax.axis_index("space")
    total_planes = planes * lax.axis_size("space")
    cells = total_planes * rows_y * rows_z
    keep = (1 - support_mask).astype(jnp.float32)
    cube_ext = with_halo(density, (("space", 0),), 1) ** 3
    motion = smooth_sweep(face_rim(displacement), forces, cube_ext, keep, STEP_ONE)
    motion = smooth_sweep(face_rim(motion), forces, cube_ext, keep, STEP_TWO)
    extended = face_rim(motion)
    case_sens = energy(extended, density)
    local_work = jnp.sum(forces * motion, axis=(1, 2, 3, 4))
    score_scale = KS_BETA / (3.0 * cells)
    scores = score_scale * lax.psum(local_work, "space")
    highest = lax.pmax(jnp.max(scores), "case")
    exponent = jnp.exp(scores - highest)
    denominator = lax.psum(jnp.sum(exponent), "case")
    weights = exponent / denominator
    ks_value = (highest + jnp.log(denominator)) / KS_BETA
    combined = lax.psum(jnp.sum(weights[:, None, None, None] * case_sens, axis=0), "case")
    product = density * combined
    rim_rows = with_halo(product, (("space", 0),), 1)
    padded_y = pad_axis(product, -2, 1)
    padded_z = pad_axis(product, -1, 1)
    neighbours = (
        rim_rows[2:]
        + rim_rows[:-2]
        + padded_y[:, 2:]
        + padded_y[:, :-2]
        + padded_z[:, :, 2:]
        + padded_z[:, :, :-2]
    )
    plane_ids = slab_index * planes + jnp.arange(planes)
    x_count = (plane_ids > 0).astype(jnp.float32) + (plane_ids < total_planes - 1).astype(
        jnp.float32
    )
    y_ids = jnp.arange(rows_y)
    y_count = (y_ids > 0).astype(jnp.float32) + (y_ids < rows_y - 1).astype(jnp.float32)
    z_ids = jnp.arange(rows_z)
    z_count = (z_ids > 0).astype(jnp.float32) + (z_ids < rows_z - 1).astype(jnp.float32)
    counts = x_count[:, None, None] + y_count[None, :, None] + z_count[None, None, :]
    filtered = (2.0 * product + neighbours) / (density * (2.0 + counts))
    scale = lax.psum(jnp.sum(-filtered), "space") / cells + 1e-06
    updated = jnp.clip(density + MOVE_LIMIT * (-filtered / scale - 1.0), DENSITY_MIN, 1.0)
    new_density = jnp.where(void_mask == 1, DENSITY_MIN, updated)
    return (motion, new_density, ks_value.reshape(1))


def solution(mesh):
    return jax.shard_map(
        body,
        mesh=mesh,
        in_specs=(
            P(("design", "case"), None, "space", None, None),
            P(("design", "case"), None, "space", None, None),
            P(("design", "space"), None, None),
            P(("design", "space"), None, None),
            P(("design", "space"), None, None),
        ),
        out_specs=(
            P(("design", "case"), None, "space", None, None),
            P(("design", "space"), None, None),
            P("design"),
        ),
        check_vma=False,
    )
```

profile of v0, /device:TPU:0, one launch (start us, length us, event | category | flops | bytes accessed | tf_op | source)
XLA Modules:
  0.0 140.1 jit_solution(4590353172492582459)
XLA Ops:
  7.2 0.7 fusion.90
  7.9 4.9 %collective-permute-start = (f32[1,16,128]{2,1,0:T(8,128)S(1)}, f32[1,16,128]{2,1,0:T(8,128)S(1)}, u32[]{:S(2)}, u32[]{:S(2)}) collective-permute-start(f32[1,16,128]{2,1,0:T(8,128)S(1)} %get-tuple-element.25), channel_id=1, source_target_pairs={{0,2},{2,4},{4,6},{6,8},{8,10},{10,12},{12,14},{1,3},{3,5},{5,7},{... | collective-permute-start | bytes 24584 | tf_op jit(solution)/shard_map/ppermute | solution.py:21
  12.8 1.3 collective-permute-start.1
  14.1 1.0 fusion.87
  15.1 1.3 collective-permute-start.2
  16.4 5.2 %collective-permute-start.3 = (f32[4,3,1,16,128]{4,3,2,1,0:T(8,128)S(1)}, f32[4,3,1,16,128]{4,3,2,1,0:T(8,128)S(1)}, u32[]{:S(2)}, u32[]{:S(2)}) collective-permute-start(f32[4,3,1,16,128]{4,3,2,1,0:T(8,128)S(1)} %get-tuple-element.12), channel_id=1, source_target_pairs={{0,2},{2,4},{4,6},{6,8},{8,10},{10,12},{12,14},{1,3},{3,5},{5,7},{... | collective-permute-start | bytes 294920 | tf_op jit(solution)/shard_map/ppermute | solution.py:21
  21.5 0.9 subtract_convert_fusion
  22.5 0.9 multiply_multiply_fusion.1
  25.0 1.5 %fusion.63 = f32[4,3,12,16,128]{4,3,2,1,0:T(8,128)S(1)} fusion(f32[4,3,12,16,128]{4,3,2,1,0:T(8,128)S(1)} %copy-done.3, f32[4,3,12,16,128]{4,3,2,1,0:T(8,128)S(1)} %copy-done, f32[4,3,1,16,128]{4,3,2,1,0:T(8,128)S(1)} %collective-permute-done.3, f32[4,3,1,16,128]{4,3,2,1,0:T(8,128)S(1)} %collective-permute-done.2, f32[12,16,128]{2,1,0:T(8,128)S(1)} %get-tuple-element.14, ...), kind=kLoop, calls=%fused_computation.82 | loop fusion | flops 7667712 | bytes 4521984 | tf_op jit(solution)/shard_map/mul | solution.py:73
  26.5 1.3 collective-permute-start.4
  27.8 6.1 %collective-permute-start.5 = (f32[4,3,1,16,128]{4,3,2,1,0:T(8,128)S(1)}, f32[4,3,1,16,128]{4,3,2,1,0:T(8,128)}, u32[]{:S(2)}, u32[]{:S(2)}) collective-permute-start(f32[4,3,1,16,128]{4,3,2,1,0:T(8,128)S(1)} %get-tuple-element.10), channel_id=1, source_target_pairs={{0,2},{2,4},{4,6},{6,8},{8,10},{10,12},{12,14},{1,3},{3,5},{5,7},{... | collective-permute-start | bytes 294920 | tf_op jit(solution)/shard_map/ppermute | solution.py:21
  34.0 1.5 %collective-permute-done.5 = f32[4,3,1,16,128]{4,3,2,1,0:T(8,128)} collective-permute-done((f32[4,3,1,16,128]{4,3,2,1,0:T(8,128)S(1)}, f32[4,3,1,16,128]{4,3,2,1,0:T(8,128)}, u32[]{:S(2)}, u32[]{:S(2)}) %collective-permute-start.5) | collective-permute-done | bytes 98336 | tf_op jit(solution)/shard_map/ppermute | solution.py:21
  35.5 2.4 %fusion.62 = f32[4,3,12,16,128]{4,3,2,1,0:T(8,128)S(1)} fusion(f32[4,3,12,16,128]{4,3,2,1,0:T(8,128)S(1)} %fusion.63, f32[4,3,12,16,128]{4,3,2,1,0:T(8,128)S(1)} %copy-done, f32[4,3,1,16,128]{4,3,2,1,0:T(8,128)} %collective-permute-done.5, f32[4,3,1,16,128]{4,3,2,1,0:T(8,128)S(1)} %collective-permute-done.4, f32[12,16,128]{2,1,0:T(8,128)S(1)} %get-tuple-element.14, ...), kind=kLoop, calls=%fused_computation.81 | loop fusion | flops 7667712 | bytes 4521984 | tf_op jit(solution)/shard_map/mul | solution.py:73
  37.9 1.3 collective-permute-start.6
  39.2 5.5 %collective-permute-start.7 = (f32[4,3,1,16,128]{4,3,2,1,0:T(8,128)S(1)}, f32[4,3,1,16,128]{4,3,2,1,0:T(8,128)S(1)}, u32[]{:S(2)}, u32[]{:S(2)}) collective-permute-start(f32[4,3,1,16,128]{4,3,2,1,0:T(8,128)S(1)} %get-tuple-element.8), channel_id=1, source_target_pairs={{0,2},{2,4},{4,6},{6,8},{8,10},{10,12},{12,14},{1,3},{3,5},{5,7},{... | collective-permute-start | bytes 294920 | tf_op jit(solution)/shard_map/ppermute | solution.py:21
  44.7 0.6 collective-permute-done.6
  45.3 2.0 %collective-permute-done.7 = f32[4,3,1,16,128]{4,3,2,1,0:T(8,128)S(1)} collective-permute-done((f32[4,3,1,16,128]{4,3,2,1,0:T(8,128)S(1)}, f32[4,3,1,16,128]{4,3,2,1,0:T(8,128)S(1)}, u32[]{:S(2)}, u32[]{:S(2)}) %collective-permute-start.7) | collective-permute-done | bytes 98336 | tf_op jit(solution)/shard_map/ppermute | solution.py:21
  47.3 1.1 multiply_reduce_fusion
  48.4 24.6 %psum.28 = f32[4]{0:T(128)S(1)} all-reduce(f32[4]{0:T(128)S(1)} %get-tuple-element.3), channel_id=1, replica_groups=mesh['design'=2,'space'=8,'case'=2] {'space'}, use_global_device_ids=true, to_apply=%region_1.2 | all-reduce | flops 4 | bytes 32 | tf_op jit(solution)/shard_map/psum | solution.py:105
  73.0 0.6 multiply_reduce_fusion.2
  73.6 3.1 %pmax.7 = f32[]{:T(128)} all-reduce(f32[]{:T(128)} %multiply_reduce_fusion.2), channel_id=1, replica_groups=mesh['design'=2,'space'=8,'case'=2] {'case'}, use_global_device_ids=true, to_apply=%region_3.4 | all-reduce | flops 1 | bytes 8 | tf_op jit(solution)/shard_map/pmax | solution.py:106
  76.7 1.3 fusion.82
  78.0 3.1 %psum.29 = f32[]{:T(128)} all-reduce(f32[]{:T(128)} %fusion.82), channel_id=1, replica_groups=mesh['design'=2,'space'=8,'case'=2] {'case'}, use_global_device_ids=true, to_apply=%region_5.6 | all-reduce | flops 1 | bytes 8 | tf_op jit(solution)/shard_map/psum | solution.py:108
  81.0 1.2 broadcast_divide_fusion
  82.2 0.7 multiply_reduce_fusion.1
  83.1 15.2 %all-reduce.12.cloned.1.call-done = f32[12,16,128]{2,1,0:T(8,128)} async-done(((f32[12,16,128]{2,1,0:T(8,128)}), f32[12,16,128]{2,1,0:T(8,128)}) %all-reduce.12.cloned.1.call-update) | async-done | bytes 98320 | tf_op jit(solution)/shard_map/psum | solution.py:111
  98.3 0.9 mul.216
  99.2 1.3 collective-permute-start.8
  100.5 4.5 %collective-permute-start.9 = (f32[1,16,128]{2,1,0:T(8,128)S(1)}, f32[1,16,128]{2,1,0:T(8,128)S(1)}, u32[]{:S(2)}, u32[]{:S(2)}) collective-permute-start(f32[1,16,128]{2,1,0:T(8,128)S(1)} %get-tuple-element.21), channel_id=1, source_target_pairs={{0,2},{2,4},{4,6},{6,8},{8,10},{10,12},{12,14},{1,3},{3,5},{5,7},{... | collective-permute-start | bytes 24584 | tf_op jit(solution)/shard_map/ppermute | solution.py:21
  106.4 0.7 fusion.83
  107.8 23.0 %psum.31 = f32[]{:T(128)} all-reduce(f32[]{:T(128)S(6)} %neg.7), channel_id=1, replica_groups=mesh['design'=2,'space'=8,'case'=2] {'space'}, use_global_device_ids=true, to_apply=%region_10.11 | all-reduce | flops 1 | bytes 8 | tf_op jit(solution)/shard_map/psum | solution.py:134
  131.4 0.7 clamp_select_fusion
  (34 shorter events, 1.9 us)
Async XLA Ops:
  7.2 91.1 %all-reduce.12.cloned.1.call-start = ((), (), s32[]{:S(2)}) async-start(), calls=%async_computation | async-start | bytes 196608 | tf_op jit(solution)/shard_map/psum | solution.py:111
  7.9 14.5 %collective-permute-start = (f32[1,16,128]{2,1,0:T(8,128)S(1)}, f32[1,16,128]{2,1,0:T(8,128)S(1)}, u32[]{:S(2)}, u32[]{:S(2)}) collective-permute-start(f32[1,16,128]{2,1,0:T(8,128)S(1)} %get-tuple-element.25), channel_id=1, source_target_pairs={{0,2},{2,4},{4,6},{6,8},{8,10},{10,12},{12,14},{1,3},{3,5},{5,7},{... | collective-permute-start | bytes 24584 | tf_op jit(solution)/shard_map/ppermute | solution.py:21
  12.8 10.6 %collective-permute-start.1 = (f32[1,16,128]{2,1,0:T(8,128)S(1)}, f32[1,16,128]{2,1,0:T(8,128)S(1)}, u32[]{:S(2)}, u32[]{:S(2)}) collective-permute-start(f32[1,16,128]{2,1,0:T(8,128)S(1)} %get-tuple-element.24), channel_id=1, source_target_pairs={{2,0},{4,2},{6,4},{8,6},{10,8},{12,10},{14,12},{3,1},{5,3},{7,5},{... | collective-permute-start | bytes 24584 | tf_op jit(solution)/shard_map/ppermute | solution.py:24
  15.1 8.7 %collective-permute-start.2 = (f32[4,3,1,16,128]{4,3,2,1,0:T(8,128)S(1)}, f32[4,3,1,16,128]{4,3,2,1,0:T(8,128)S(1)}, u32[]{:S(2)}, u32[]{:S(2)}) collective-permute-start(f32[4,3,1,16,128]{4,3,2,1,0:T(8,128)S(1)} %get-tuple-element.11), channel_id=1, source_target_pairs={{2,0},{4,2},{6,4},{8,6},{10,8},{12,10},{14,12},{3,1},{5,3},{7,5},{... | collective-permute-start | bytes 294920 | tf_op jit(solution)/shard_map/ppermute | solution.py:24
  16.4 7.7 %collective-permute-start.3 = (f32[4,3,1,16,128]{4,3,2,1,0:T(8,128)S(1)}, f32[4,3,1,16,128]{4,3,2,1,0:T(8,128)S(1)}, u32[]{:S(2)}, u32[]{:S(2)}) collective-permute-start(f32[4,3,1,16,128]{4,3,2,1,0:T(8,128)S(1)} %get-tuple-element.12), channel_id=1, source_target_pairs={{0,2},{2,4},{4,6},{6,8},{8,10},{10,12},{12,14},{1,3},{3,5},{5,7},{... | collective-permute-start | bytes 294920 | tf_op jit(solution)/shard_map/ppermute | solution.py:21
  23.4 1.3 copy-start.3
  23.4 1.6 %copy-start = (f32[4,3,12,16,128]{4,3,2,1,0:T(8,128)S(1)}, f32[4,3,12,16,128]{4,3,2,1,0:T(8,128)}, u32[]{:S(2)}) copy-start(f32[4,3,12,16,128]{4,3,2,1,0:T(8,128)} %param.6) | copy-start | bytes 3538948
  26.5 7.4 %collective-permute-start.4 = (f32[4,3,1,16,128]{4,3,2,1,0:T(8,128)S(1)}, f32[4,3,1,16,128]{4,3,2,1,0:T(8,128)S(1)}, u32[]{:S(2)}, u32[]{:S(2)}) collective-permute-start(f32[4,3,1,16,128]{4,3,2,1,0:T(8,128)S(1)} %get-tuple-element.9), channel_id=1, source_target_pairs={{2,0},{4,2},{6,4},{8,6},{10,8},{12,10},{14,12},{3,1},{5,3},{7,5},{... | collective-permute-start | bytes 294920 | tf_op jit(solution)/shard_map/ppermute | solution.py:24
  27.8 7.6 %collective-permute-start.5 = (f32[4,3,1,16,128]{4,3,2,1,0:T(8,128)S(1)}, f32[4,3,1,16,128]{4,3,2,1,0:T(8,128)}, u32[]{:S(2)}, u32[]{:S(2)}) collective-permute-start(f32[4,3,1,16,128]{4,3,2,1,0:T(8,128)S(1)} %get-tuple-element.10), channel_id=1, source_target_pairs={{0,2},{2,4},{4,6},{6,8},{8,10},{10,12},{12,14},{1,3},{3,5},{5,7},{... | collective-permute-start | bytes 294920 | tf_op jit(solution)/shard_map/ppermute | solution.py:21
  37.9 10.5 %copy-start.1 = (f32[4,3,12,16,128]{4,3,2,1,0:T(8,128)}, f32[4,3,12,16,128]{4,3,2,1,0:T(8,128)S(1)}, u32[]{:S(2)}) copy-start(f32[4,3,12,16,128]{4,3,2,1,0:T(8,128)S(1)} %fusion.62) | copy-start | bytes 3538948
  37.9 7.4 %collective-permute-start.6 = (f32[4,3,1,16,128]{4,3,2,1,0:T(8,128)S(1)}, f32[4,3,1,16,128]{4,3,2,1,0:T(8,128)S(1)}, u32[]{:S(2)}, u32[]{:S(2)}) collective-permute-start(f32[4,3,1,16,128]{4,3,2,1,0:T(8,128)S(1)} %get-tuple-element.7), channel_id=1, source_target_pairs={{2,0},{4,2},{6,4},{8,6},{10,8},{12,10},{14,12},{3,1},{5,3},{7,5},{... | collective-permute-start | bytes 294920 | tf_op jit(solution)/shard_map/ppermute | solution.py:24
  39.2 8.1 %collective-permute-start.7 = (f32[4,3,1,16,128]{4,3,2,1,0:T(8,128)S(1)}, f32[4,3,1,16,128]{4,3,2,1,0:T(8,128)S(1)}, u32[]{:S(2)}, u32[]{:S(2)}) collective-permute-start(f32[4,3,1,16,128]{4,3,2,1,0:T(8,128)S(1)} %get-tuple-element.8), channel_id=1, source_target_pairs={{0,2},{2,4},{4,6},{6,8},{8,10},{10,12},{12,14},{1,3},{3,5},{5,7},{... | collective-permute-start | bytes 294920 | tf_op jit(solution)/shard_map/ppermute | solution.py:21
  44.7 53.6 %copy-start.2 = (f32[12,16,128]{2,1,0:T(8,128)S(1)}, f32[12,16,128]{2,1,0:T(8,128)}, u32[]{:S(2)}) copy-start(f32[12,16,128]{2,1,0:T(8,128)} %param.7) | copy-start | bytes 294916
  48.4 83.1 %copy-start.4 = (s32[12,16,128]{2,1,0:T(8,128)S(1)}, s32[12,16,128]{2,1,0:T(8,128)}, u32[]{:S(2)}) copy-start(s32[12,16,128]{2,1,0:T(8,128)} %param.9) | copy-start | bytes 294916
  99.2 7.1 %collective-permute-start.8 = (f32[1,16,128]{2,1,0:T(8,128)S(1)}, f32[1,16,128]{2,1,0:T(8,128)S(1)}, u32[]{:S(2)}, u32[]{:S(2)}) collective-permute-start(f32[1,16,128]{2,1,0:T(8,128)S(1)} %get-tuple-element.20), channel_id=1, source_target_pairs={{2,0},{4,2},{6,4},{8,6},{10,8},{12,10},{14,12},{3,1},{5,3},{7,5},{... | collective-permute-start | bytes 24584 | tf_op jit(solution)/shard_map/ppermute | solution.py:24
  100.5 5.9 %collective-permute-start.9 = (f32[1,16,128]{2,1,0:T(8,128)S(1)}, f32[1,16,128]{2,1,0:T(8,128)S(1)}, u32[]{:S(2)}, u32[]{:S(2)}) collective-permute-start(f32[1,16,128]{2,1,0:T(8,128)S(1)} %get-tuple-element.21), channel_id=1, source_target_pairs={{0,2},{2,4},{4,6},{6,8},{8,10},{10,12},{12,14},{1,3},{3,5},{5,7},{... | collective-permute-start | bytes 24584 | tf_op jit(solution)/shard_map/ppermute | solution.py:21
Sparse Core Ops, SparseCore 0:
  83.1 15.0 all-reduce.11
where the time goes:
time: 141 us; the launch traced here: 140 us
  blocking collectives  53.8 us (38%)
  starting transfers between devices  32.6 us (23%)
  waiting for transfers between devices  19.8 us (14%)
  between operations  18 us (13%)
  other arithmetic  13.2 us (9%)
  local copies, waits for them, and re-layouts  2.71 us (2%)
    ppermute x5, starting transfers between devices, with_halo(): lax.ppermute(lax.slice_in_dim(block, block.shape[dim] - width, None, axis...  26.1 us
    psum x1, blocking collectives, body(): scores = score_scale * lax.psum(local_work, 'space')  24.6 us
    psum x1, blocking collectives, body(): scale = lax.psum(jnp.sum(-filtered), 'space') / cells + 1e-06  23 us
    psum x1, waiting for transfers between devices, body(): lax.psum(jnp.sum(weights[:, None, None, None] * case_sens, axis=0), 'case')  15.2 us
    ppermute x5, starting transfers between devices, with_halo(): lax.ppermute(lax.slice_in_dim(block, 0, width, axis=dim), axis, backward)  6.46 us
    ppermute x5, waiting for transfers between devices, with_halo(): lax.ppermute(lax.slice_in_dim(block, block.shape[dim] - width, None, axis...  3.92 us
    mul x2, other arithmetic, smooth_sweep(): return keep * (centre + factor * (loads - applied) / diagonal)  3.82 us
    pmax x1, blocking collectives, body(): highest = lax.pmax(jnp.max(scores), 'case')  3.08 us
  transfers between devices with their start and end apart: 11, of which 6 were waited for; matrix products, arithmetic and copies ran while one was open for 2% of the time, Pallas kernels for 0%

commit v1 on v0

--- a/solution.py
+++ b/solution.py
@@ -11,6 +11,10 @@
 DENSITY_MIN = 0.001
 STEP_ONE = 1.0 / (1.15 + 0.85 * math.cos(math.pi / 4))
 STEP_TWO = 1.0 / (1.15 - 0.85 * math.cos(math.pi / 4))
+
+
+def try_all_copies(arr_in):
+    return jnp.sum(jax.lax.all_gather(arr_in, axis_name="case"), axis=0)
 
 
 def with_halo(block, sides, width):
@@ -108,7 +112,7 @@
     denominator = lax.psum(jnp.sum(exponent), "case")
     weights = exponent / denominator
     ks_value = (highest + jnp.log(denominator)) / KS_BETA
-    combined = lax.psum(jnp.sum(weights[:, None, None, None] * case_sens, axis=0), "case")
+    combined = try_all_copies(jnp.sum(weights[:, None, None, None] * case_sens, axis=0))
     product = density * combined
     rim_rows = with_halo(product, (("space", 0),), 1)
     padded_y = pad_axis(product, -2, 1)

time: 141 us -> 110 us (0.78)
  waiting for transfers between devices: 19.8 us -> 4.53 us
  between operations: 18 us -> 4.73 us
    psum x1 -> x0, waiting for transfers between devices: 15.2 us -> none  [body(): lax.psum(jnp.sum(weights[:, None, None, None] * case_sens, axis=0), 'case')]
    psum x1, blocking collectives: 23 us -> 19.9 us  [body(): scale = lax.psum(jnp.sum(-filtered), 'space') / cells + 1e-06]
    all_gather x0 -> x1, blocking collectives: none -> 1.95 us  [try_all_copies(): return jnp.sum(jax.lax.all_gather(arr_in, axis_name='case'), axis=0)]
  transfers between devices with their start and end apart: 11 -> 10, of which waited for: 6 -> 4; matrix products, arithmetic and copies ran while one was open for 2% -> 3% of each run, Pallas kernels for 0% -> 0%
where the time goes in v1:
time: 110 us; the launch traced here: 109 us
  blocking collectives  52.6 us (48%)
  starting transfers between devices  32.6 us (30%)
  other arithmetic  11.8 us (11%)
  between operations  4.73 us (4%)
  waiting for transfers between devices  4.53 us (4%)
  local copies, waits for them, and re-layouts  2.71 us (2%)
    ppermute x5, starting transfers between devices, with_halo(): lax.ppermute(lax.slice_in_dim(block, block.shape[dim] - width, None, axis...  26.1 us
    psum x1, blocking collectives, body(): scores = score_scale * lax.psum(local_work, 'space')  24.6 us
    psum x1, blocking collectives, body(): scale = lax.psum(jnp.sum(-filtered), 'space') / cells + 1e-06  19.9 us
    ppermute x5, starting transfers between devices, with_halo(): lax.ppermute(lax.slice_in_dim(block, 0, width, axis=dim), axis, backward)  6.46 us
    ppermute x5, waiting for transfers between devices, with_halo(): lax.ppermute(lax.slice_in_dim(block, block.shape[dim] - width, None, axis...  3.84 us
    mul x2, other arithmetic, smooth_sweep(): return keep * (centre + factor * (loads - applied) / diagonal)  3.82 us
    psum x1, blocking collectives, body(): denominator = lax.psum(jnp.sum(exponent), 'case')  3.08 us
    pmax x1, blocking collectives, body(): highest = lax.pmax(jnp.max(scores), 'case')  3.08 us
  transfers between devices with their start and end apart: 10, of which 4 were waited for; matrix products, arithmetic and copies ran while one was open for 3% of the time, Pallas kernels for 0%

profile of v1, /device:TPU:0, one launch (start us, length us, event | category | flops | bytes accessed | tf_op | source)
XLA Modules:
  0.0 108.9 jit_solution(18037301788106213618)
XLA Ops:
  0.6 0.7 fusion.90
  1.3 4.9 %collective-permute-start = (f32[1,16,128]{2,1,0:T(8,128)S(1)}, f32[1,16,128]{2,1,0:T(8,128)S(1)}, u32[]{:S(2)}, u32[]{:S(2)}) collective-permute-start(f32[1,16,128]{2,1,0:T(8,128)S(1)} %get-tuple-element.25), channel_id=1, source_target_pairs={{0,2},{2,4},{4,6},{6,8},{8,10},{10,12},{12,14},{1,3},{3,5},{5,7},{... | collective-permute-start | bytes 24584 | tf_op jit(solution)/shard_map/ppermute | solution.py:25
  6.2 1.3 %collective-permute-start.1 = (f32[1,16,128]{2,1,0:T(8,128)S(1)}, f32[1,16,128]{2,1,0:T(8,128)S(1)}, u32[]{:S(2)}, u32[]{:S(2)}) collective-permute-start(f32[1,16,128]{2,1,0:T(8,128)S(1)} %get-tuple-element.24), channel_id=1, source_target_pairs={{2,0},{4,2},{6,4},{8,6},{10,8},{12,10},{14,12},{3,1},{5,3},{7,5},{... | collective-permute-start | bytes 24584 | tf_op jit(solution)/shard_map/ppermute | solution.py:28
  7.5 1.0 fusion.87
  8.5 1.3 %collective-permute-start.2 = (f32[4,3,1,16,128]{4,3,2,1,0:T(8,128)S(1)}, f32[4,3,1,16,128]{4,3,2,1,0:T(8,128)S(1)}, u32[]{:S(2)}, u32[]{:S(2)}) collective-permute-start(f32[4,3,1,16,128]{4,3,2,1,0:T(8,128)S(1)} %get-tuple-element.11), channel_id=1, source_target_pairs={{2,0},{4,2},{6,4},{8,6},{10,8},{12,10},{14,12},{3,1},{5,3},{7,5},{... | collective-permute-start | bytes 294920 | tf_op jit(solution)/shard_map/ppermute | solution.py:28
  9.8 5.2 %collective-permute-start.3 = (f32[4,3,1,16,128]{4,3,2,1,0:T(8,128)S(1)}, f32[4,3,1,16,128]{4,3,2,1,0:T(8,128)S(1)}, u32[]{:S(2)}, u32[]{:S(2)}) collective-permute-start(f32[4,3,1,16,128]{4,3,2,1,0:T(8,128)S(1)} %get-tuple-element.12), channel_id=1, source_target_pairs={{0,2},{2,4},{4,6},{6,8},{8,10},{10,12},{12,14},{1,3},{3,5},{5,7},{... | collective-permute-start | bytes 294920 | tf_op jit(solution)/shard_map/ppermute | solution.py:25
  15.0 0.9 subtract_convert_fusion
  15.9 0.9 multiply_multiply_fusion.1
  17.5 0.6 copy-done.3
  18.1 0.4 copy-done
  18.5 1.5 %fusion.63 = f32[4,3,12,16,128]{4,3,2,1,0:T(8,128)S(1)} fusion(f32[4,3,12,16,128]{4,3,2,1,0:T(8,128)S(1)} %copy-done.3, f32[4,3,12,16,128]{4,3,2,1,0:T(8,128)S(1)} %copy-done, f32[4,3,1,16,128]{4,3,2,1,0:T(8,128)S(1)} %collective-permute-done.3, f32[4,3,1,16,128]{4,3,2,1,0:T(8,128)S(1)} %collective-permute-done.2, f32[12,16,128]{2,1,0:T(8,128)S(1)} %get-tuple-element.14, ...), kind=kLoop, calls=%fused_computation.82 | loop fusion | flops 7667712 | bytes 4521984 | tf_op jit(solution)/shard_map/mul | solution.py:77
  20.0 1.3 %collective-permute-start.4 = (f32[4,3,1,16,128]{4,3,2,1,0:T(8,128)S(1)}, f32[4,3,1,16,128]{4,3,2,1,0:T(8,128)S(1)}, u32[]{:S(2)}, u32[]{:S(2)}) collective-permute-start(f32[4,3,1,16,128]{4,3,2,1,0:T(8,128)S(1)} %get-tuple-element.9), channel_id=1, source_target_pairs={{2,0},{4,2},{6,4},{8,6},{10,8},{12,10},{14,12},{3,1},{5,3},{7,5},{... | collective-permute-start | bytes 294920 | tf_op jit(solution)/shard_map/ppermute | solution.py:28
  21.3 6.1 %collective-permute-start.5 = (f32[4,3,1,16,128]{4,3,2,1,0:T(8,128)S(1)}, f32[4,3,1,16,128]{4,3,2,1,0:T(8,128)}, u32[]{:S(2)}, u32[]{:S(2)}) collective-permute-start(f32[4,3,1,16,128]{4,3,2,1,0:T(8,128)S(1)} %get-tuple-element.10), channel_id=1, source_target_pairs={{0,2},{2,4},{4,6},{6,8},{8,10},{10,12},{12,14},{1,3},{3,5},{5,7},{... | collective-permute-start | bytes 294920 | tf_op jit(solution)/shard_map/ppermute | solution.py:25
  27.4 1.5 %collective-permute-done.5 = f32[4,3,1,16,128]{4,3,2,1,0:T(8,128)} collective-permute-done((f32[4,3,1,16,128]{4,3,2,1,0:T(8,128)S(1)}, f32[4,3,1,16,128]{4,3,2,1,0:T(8,128)}, u32[]{:S(2)}, u32[]{:S(2)}) %collective-permute-start.5) | collective-permute-done | bytes 98336 | tf_op jit(solution)/shard_map/ppermute | solution.py:25
  28.9 2.4 %fusion.62 = f32[4,3,12,16,128]{4,3,2,1,0:T(8,128)S(1)} fusion(f32[4,3,12,16,128]{4,3,2,1,0:T(8,128)S(1)} %fusion.63, f32[4,3,12,16,128]{4,3,2,1,0:T(8,128)S(1)} %copy-done, f32[4,3,1,16,128]{4,3,2,1,0:T(8,128)} %collective-permute-done.5, f32[4,3,1,16,128]{4,3,2,1,0:T(8,128)S(1)} %collective-permute-done.4, f32[12,16,128]{2,1,0:T(8,128)S(1)} %get-tuple-element.14, ...), kind=kLoop, calls=%fused_computation.81 | loop fusion | flops 7667712 | bytes 4521984 | tf_op jit(solution)/shard_map/mul | solution.py:77
  31.3 1.3 %collective-permute-start.6 = (f32[4,3,1,16,128]{4,3,2,1,0:T(8,128)S(1)}, f32[4,3,1,16,128]{4,3,2,1,0:T(8,128)S(1)}, u32[]{:S(2)}, u32[]{:S(2)}) collective-permute-start(f32[4,3,1,16,128]{4,3,2,1,0:T(8,128)S(1)} %get-tuple-element.7), channel_id=1, source_target_pairs={{2,0},{4,2},{6,4},{8,6},{10,8},{12,10},{14,12},{3,1},{5,3},{7,5},{... | collective-permute-start | bytes 294920 | tf_op jit(solution)/shard_map/ppermute | solution.py:28
  32.6 5.5 %collective-permute-start.7 = (f32[4,3,1,16,128]{4,3,2,1,0:T(8,128)S(1)}, f32[4,3,1,16,128]{4,3,2,1,0:T(8,128)S(1)}, u32[]{:S(2)}, u32[]{:S(2)}) collective-permute-start(f32[4,3,1,16,128]{4,3,2,1,0:T(8,128)S(1)} %get-tuple-element.8), channel_id=1, source_target_pairs={{0,2},{2,4},{4,6},{6,8},{8,10},{10,12},{12,14},{1,3},{3,5},{5,7},{... | collective-permute-start | bytes 294920 | tf_op jit(solution)/shard_map/ppermute | solution.py:25
  38.1 0.6 collective-permute-done.6
  38.7 2.0 %collective-permute-done.7 = f32[4,3,1,16,128]{4,3,2,1,0:T(8,128)S(1)} collective-permute-done((f32[4,3,1,16,128]{4,3,2,1,0:T(8,128)S(1)}, f32[4,3,1,16,128]{4,3,2,1,0:T(8,128)S(1)}, u32[]{:S(2)}, u32[]{:S(2)}) %collective-permute-start.7) | collective-permute-done | bytes 98336 | tf_op jit(solution)/shard_map/ppermute | solution.py:25
  40.7 1.1 multiply_reduce_fusion
  41.8 24.6 %psum.21 = f32[4]{0:T(128)S(1)} all-reduce(f32[4]{0:T(128)S(1)} %get-tuple-element.3), channel_id=1, replica_groups=mesh['design'=2,'space'=8,'case'=2] {'space'}, use_global_device_ids=true, to_apply=%region_1.2 | all-reduce | flops 4 | bytes 32 | tf_op jit(solution)/shard_map/psum | solution.py:109
  66.5 0.6 multiply_reduce_fusion.2
  67.1 3.1 %pmax.7 = f32[]{:T(128)} all-reduce(f32[]{:T(128)} %multiply_reduce_fusion.2), channel_id=1, replica_groups=mesh['design'=2,'space'=8,'case'=2] {'case'}, use_global_device_ids=true, to_apply=%region_3.4 | all-reduce | flops 1 | bytes 8 | tf_op jit(solution)/shard_map/pmax | solution.py:110
  70.1 1.3 %fusion.82 = f32[]{:T(128)} fusion(f32[]{:T(128)} %pmax.7, f32[4]{0:T(128)S(1)} %psum.21), kind=kLoop, calls=%fused_computation.131 | loop fusion | flops 11 | bytes 24 | tf_op jit(solution)/shard_map/reduce_sum | solution.py:112
  71.5 3.1 %psum.22 = f32[]{:T(128)} all-reduce(f32[]{:T(128)} %fusion.82), channel_id=1, replica_groups=mesh['design'=2,'space'=8,'case'=2] {'case'}, use_global_device_ids=true, to_apply=%region_5.6 | all-reduce | flops 1 | bytes 8 | tf_op jit(solution)/shard_map/psum | solution.py:112
  74.5 1.3 %broadcast_divide_fusion = f32[4]{0:T(128)S(1)} fusion(f32[]{:T(128)} %psum.22, f32[]{:T(128)} %pmax.7, f32[4]{0:T(128)S(1)} %psum.21), kind=kLoop, calls=%fused_computation.130 | loop fusion | flops 12 | bytes 40 | tf_op jit(solution)/shard_map/div | solution.py:113
  75.9 1.9 %all-gather = f32[24,16,128]{2,1,0:T(8,128)S(1)} all-gather(f32[12,16,128]{2,1,0:T(8,128)S(1)} %multiply_reduce_fusion.1), channel_id=2, replica_groups=mesh['design'=2,'space'=8,'case'=2] {'case'}, dimensions={0}, use_global_device_ids=true | all-gather | bytes 294912 | tf_op jit(solution)/shard_map/all_gather | solution.py:17
  78.0 1.3 %collective-permute-start.8 = (f32[1,16,128]{2,1,0:T(8,128)S(1)}, f32[1,16,128]{2,1,0:T(8,128)S(1)}, u32[]{:S(2)}, u32[]{:S(2)}) collective-permute-start(f32[1,16,128]{2,1,0:T(8,128)S(1)} %get-tuple-element.20), channel_id=1, source_target_pairs={{2,0},{4,2},{6,4},{8,6},{10,8},{12,10},{14,12},{3,1},{5,3},{7,5},{... | collective-permute-start | bytes 24584 | tf_op jit(solution)/shard_map/ppermute | solution.py:28
  79.3 4.5 %collective-permute-start.9 = (f32[1,16,128]{2,1,0:T(8,128)S(1)}, f32[1,16,128]{2,1,0:T(8,128)S(1)}, u32[]{:S(2)}, u32[]{:S(2)}) collective-permute-start(f32[1,16,128]{2,1,0:T(8,128)S(1)} %get-tuple-element.21), channel_id=1, source_target_pairs={{0,2},{2,4},{4,6},{6,8},{8,10},{10,12},{12,14},{1,3},{3,5},{5,7},{... | collective-permute-start | bytes 24584 | tf_op jit(solution)/shard_map/ppermute | solution.py:25
  85.2 0.7 fusion.83
  86.6 19.9 %psum.23 = f32[]{:T(128)} all-reduce(f32[]{:T(128)S(6)} %neg.7), channel_id=1, replica_groups=mesh['design'=2,'space'=8,'case'=2] {'space'}, use_global_device_ids=true, to_apply=%region_10.11 | all-reduce | flops 1 | bytes 8 | tf_op jit(solution)/shard_map/psum | solution.py:138
  107.1 0.7 clamp_select_fusion
  (33 shorter events, 0.9 us)
Async XLA Ops:
  1.3 14.5 %collective-permute-start = (f32[1,16,128]{2,1,0:T(8,128)S(1)}, f32[1,16,128]{2,1,0:T(8,128)S(1)}, u32[]{:S(2)}, u32[]{:S(2)}) collective-permute-start(f32[1,16,128]{2,1,0:T(8,128)S(1)} %get-tuple-element.25), channel_id=1, source_target_pairs={{0,2},{2,4},{4,6},{6,8},{8,10},{10,12},{12,14},{1,3},{3,5},{5,7},{... | collective-permute-start | bytes 24584 | tf_op jit(solution)/shard_map/ppermute | solution.py:25
  6.2 10.6 %collective-permute-start.1 = (f32[1,16,128]{2,1,0:T(8,128)S(1)}, f32[1,16,128]{2,1,0:T(8,128)S(1)}, u32[]{:S(2)}, u32[]{:S(2)}) collective-permute-start(f32[1,16,128]{2,1,0:T(8,128)S(1)} %get-tuple-element.24), channel_id=1, source_target_pairs={{2,0},{4,2},{6,4},{8,6},{10,8},{12,10},{14,12},{3,1},{5,3},{7,5},{... | collective-permute-start | bytes 24584 | tf_op jit(solution)/shard_map/ppermute | solution.py:28
  8.5 8.7 %collective-permute-start.2 = (f32[4,3,1,16,128]{4,3,2,1,0:T(8,128)S(1)}, f32[4,3,1,16,128]{4,3,2,1,0:T(8,128)S(1)}, u32[]{:S(2)}, u32[]{:S(2)}) collective-permute-start(f32[4,3,1,16,128]{4,3,2,1,0:T(8,128)S(1)} %get-tuple-element.11), channel_id=1, source_target_pairs={{2,0},{4,2},{6,4},{8,6},{10,8},{12,10},{14,12},{3,1},{5,3},{7,5},{... | collective-permute-start | bytes 294920 | tf_op jit(solution)/shard_map/ppermute | solution.py:28
  9.8 7.7 %collective-permute-start.3 = (f32[4,3,1,16,128]{4,3,2,1,0:T(8,128)S(1)}, f32[4,3,1,16,128]{4,3,2,1,0:T(8,128)S(1)}, u32[]{:S(2)}, u32[]{:S(2)}) collective-permute-start(f32[4,3,1,16,128]{4,3,2,1,0:T(8,128)S(1)} %get-tuple-element.12), channel_id=1, source_target_pairs={{0,2},{2,4},{4,6},{6,8},{8,10},{10,12},{12,14},{1,3},{3,5},{5,7},{... | collective-permute-start | bytes 294920 | tf_op jit(solution)/shard_map/ppermute | solution.py:25
  16.8 1.3 %copy-start.3 = (f32[4,3,12,16,128]{4,3,2,1,0:T(8,128)S(1)}, f32[4,3,12,16,128]{4,3,2,1,0:T(8,128)}, u32[]{:S(2)}) copy-start(f32[4,3,12,16,128]{4,3,2,1,0:T(8,128)} %param.5) | copy-start | bytes 3538948
  16.9 1.6 %copy-start = (f32[4,3,12,16,128]{4,3,2,1,0:T(8,128)S(1)}, f32[4,3,12,16,128]{4,3,2,1,0:T(8,128)}, u32[]{:S(2)}) copy-start(f32[4,3,12,16,128]{4,3,2,1,0:T(8,128)} %param.6) | copy-start | bytes 3538948
  20.0 7.4 %collective-permute-start.4 = (f32[4,3,1,16,128]{4,3,2,1,0:T(8,128)S(1)}, f32[4,3,1,16,128]{4,3,2,1,0:T(8,128)S(1)}, u32[]{:S(2)}, u32[]{:S(2)}) collective-permute-start(f32[4,3,1,16,128]{4,3,2,1,0:T(8,128)S(1)} %get-tuple-element.9), channel_id=1, source_target_pairs={{2,0},{4,2},{6,4},{8,6},{10,8},{12,10},{14,12},{3,1},{5,3},{7,5},{... | collective-permute-start | bytes 294920 | tf_op jit(solution)/shard_map/ppermute | solution.py:28
  21.3 7.6 %collective-permute-start.5 = (f32[4,3,1,16,128]{4,3,2,1,0:T(8,128)S(1)}, f32[4,3,1,16,128]{4,3,2,1,0:T(8,128)}, u32[]{:S(2)}, u32[]{:S(2)}) collective-permute-start(f32[4,3,1,16,128]{4,3,2,1,0:T(8,128)S(1)} %get-tuple-element.10), channel_id=1, source_target_pairs={{0,2},{2,4},{4,6},{6,8},{8,10},{10,12},{12,14},{1,3},{3,5},{5,7},{... | collective-permute-start | bytes 294920 | tf_op jit(solution)/shard_map/ppermute | solution.py:25
  31.3 10.5 %copy-start.1 = (f32[4,3,12,16,128]{4,3,2,1,0:T(8,128)}, f32[4,3,12,16,128]{4,3,2,1,0:T(8,128)S(1)}, u32[]{:S(2)}) copy-start(f32[4,3,12,16,128]{4,3,2,1,0:T(8,128)S(1)} %fusion.62) | copy-start | bytes 3538948
  31.3 7.4 %collective-permute-start.6 = (f32[4,3,1,16,128]{4,3,2,1,0:T(8,128)S(1)}, f32[4,3,1,16,128]{4,3,2,1,0:T(8,128)S(1)}, u32[]{:S(2)}, u32[]{:S(2)}) collective-permute-start(f32[4,3,1,16,128]{4,3,2,1,0:T(8,128)S(1)} %get-tuple-element.7), channel_id=1, source_target_pairs={{2,0},{4,2},{6,4},{8,6},{10,8},{12,10},{14,12},{3,1},{5,3},{7,5},{... | collective-permute-start | bytes 294920 | tf_op jit(solution)/shard_map/ppermute | solution.py:28
  32.6 8.1 %collective-permute-start.7 = (f32[4,3,1,16,128]{4,3,2,1,0:T(8,128)S(1)}, f32[4,3,1,16,128]{4,3,2,1,0:T(8,128)S(1)}, u32[]{:S(2)}, u32[]{:S(2)}) collective-permute-start(f32[4,3,1,16,128]{4,3,2,1,0:T(8,128)S(1)} %get-tuple-element.8), channel_id=1, source_target_pairs={{0,2},{2,4},{4,6},{6,8},{8,10},{10,12},{12,14},{1,3},{3,5},{5,7},{... | collective-permute-start | bytes 294920 | tf_op jit(solution)/shard_map/ppermute | solution.py:25
  41.8 36.1 %copy-start.2 = (f32[12,16,128]{2,1,0:T(8,128)S(1)}, f32[12,16,128]{2,1,0:T(8,128)}, u32[]{:S(2)}) copy-start(f32[12,16,128]{2,1,0:T(8,128)} %param.7) | copy-start | bytes 294916
  41.8 65.3 %copy-start.4 = (s32[12,16,128]{2,1,0:T(8,128)S(1)}, s32[12,16,128]{2,1,0:T(8,128)}, u32[]{:S(2)}) copy-start(s32[12,16,128]{2,1,0:T(8,128)} %param.9) | copy-start | bytes 294916
  78.0 7.2 %collective-permute-start.8 = (f32[1,16,128]{2,1,0:T(8,128)S(1)}, f32[1,16,128]{2,1,0:T(8,128)S(1)}, u32[]{:S(2)}, u32[]{:S(2)}) collective-permute-start(f32[1,16,128]{2,1,0:T(8,128)S(1)} %get-tuple-element.20), channel_id=1, source_target_pairs={{2,0},{4,2},{6,4},{8,6},{10,8},{12,10},{14,12},{3,1},{5,3},{7,5},{... | collective-permute-start | bytes 24584 | tf_op jit(solution)/shard_map/ppermute | solution.py:28
  79.3 5.9 %collective-permute-start.9 = (f32[1,16,128]{2,1,0:T(8,128)S(1)}, f32[1,16,128]{2,1,0:T(8,128)S(1)}, u32[]{:S(2)}, u32[]{:S(2)}) collective-permute-start(f32[1,16,128]{2,1,0:T(8,128)S(1)} %get-tuple-element.21), channel_id=1, source_target_pairs={{0,2},{2,4},{4,6},{6,8},{8,10},{10,12},{12,14},{1,3},{3,5},{5,7},{... | collective-permute-start | bytes 24584 | tf_op jit(solution)/shard_map/ppermute | solution.py:25
